TPU v7x, 256 devices: a whole 4x4x8 slice. The times are simulated.
256 devices in a mesh: row: 16 (over z, x_lo), col: 16 (over y, x_hi, core).
Axes of the slice: x: 4 (x_hi: 2, x_lo: 2; x = x_hi * 2 + x_lo), y: 4, z: 8, core: 2. Of those that a mesh axis runs over, the one named last changes fastest.
Arguments:
- pair: bfloat16 [512, 512, 128], P('row', 'col'), may hold values from -6 to 6
- pair_mask: int32 [512, 512], P('row', 'col'), may hold values from 0 to 1, as said below
- proj_weight: bfloat16 [128, 640], replicated, may hold values from -0.5 to 0.5
- out_weight: bfloat16 [128, 128], replicated, may hold values from -0.5 to 0.5
- in_gain: float32 [128], replicated, may hold values from 0.5 to 1.5
- out_gain: float32 [128], replicated, may hold values from 0.5 to 1.5
- cotangent: bfloat16 [512, 512, 128], P('row', 'col'), may hold values from -6 to 6
Outputs:
- d_pair: float32 [512, 512, 128], P('row', 'col')
- d_proj_weight: float32 [128, 640], replicated
- d_out_weight: float32 [128, 128], replicated
- d_in_gain: float32 [128], replicated
- d_out_gain: float32 [128], replicated
Inputs may be any that keep to these rules, and one draw needn't show every extreme that they name: pair_mask[i, j] is the product of a 0/1 flag of token i and the same flag of token j.
All inputs are finite; a program needn't handle non-finite values.
Results may differ from a plain program's by a relative error of at most 0.019.
Values may be sent and summed in bfloat16 or wider, within the bound.
A program may use at most 128 MiB of HBM per device.

v0:
```python
import jax
import jax.numpy as jnp
from jax import lax
from jax.sharding import PartitionSpec as P


def normalize(values):
    average = jnp.mean(values, axis=-1, keepdims=True)
    centred = values - average
    spread = jnp.mean(centred * centred, axis=-1, keepdims=True)
    inverse = lax.rsqrt(spread + 1e-05)
    return (centred * inverse, inverse)


def layer_back(grad_hat, normed, inverse):
    first_mean = jnp.mean(grad_hat, axis=-1, keepdims=True)
    second_mean = jnp.mean(grad_hat * normed, axis=-1, keepdims=True)
    return (grad_hat - first_mean - normed * second_mean) * inverse


AXES = ("row", "col")


def exchange(x):
    return lax.all_to_all(x, AXES, split_axis=0, concat_axis=0, tiled=True)


def body(pair, pair_mask, proj_weight, out_weight, in_gain, out_gain, cotangent):
    t = pair.shape[0]
    half_t = t // 2
    channels = pair.shape[2]
    rows = lax.axis_size("row")
    cols = lax.axis_size("col")
    total = t * rows
    half = lax.rem(lax.axis_index("col"), 2)
    normed, inverse = normalize(pair.astype(jnp.float32))
    zn = (normed * in_gain).astype(jnp.bfloat16)
    linear = jnp.einsum("ijc,ce->ije", zn, proj_weight, preferred_element_type=jnp.float32)
    proj_left = linear[..., 0:channels]
    gate_left = linear[..., channels : 2 * channels]
    proj_right = linear[..., 2 * channels : 3 * channels]
    gate_right = linear[..., 3 * channels : 4 * channels]
    gate_out = linear[..., 4 * channels :]
    mask_f = pair_mask.astype(jnp.float32)[..., None]
    sig_left = jax.nn.sigmoid(gate_left)
    sig_right = jax.nn.sigmoid(gate_right)
    left = (mask_f * sig_left * proj_left).astype(jnp.bfloat16)
    right = (mask_f * sig_right * proj_right).astype(jnp.bfloat16)

    def out_full(x):
        x = jnp.transpose(x, (2, 0, 1)).reshape(channels, 1, t * t)
        return jnp.broadcast_to(x, (channels, 2, t * t)).reshape(2 * channels, t * t)

    def matrix(x):
        return x.reshape(rows, cols, t, t).transpose(0, 2, 1, 3).reshape(rows * t, cols * t)

    def pick(x):
        x = x.reshape(x.shape[0], -1, 2, half_t)
        return lax.dynamic_index_in_dim(x, half, 2, keepdims=False).reshape(x.shape[0], -1)

    sent = exchange(jnp.concatenate([out_full(left), out_full(right)], axis=1))
    left_c = matrix(sent[:, : t * t])
    right_c = matrix(sent[:, t * t :])
    tri_c = jnp.einsum("ki,kj->ij", pick(left_c), right_c, preferred_element_type=jnp.float32)
    tri_c = tri_c.astype(jnp.bfloat16).reshape(rows, half_t, cols, t).transpose(0, 2, 1, 3)
    tri = exchange(tri_c.reshape(rows * cols, half_t * t))
    triangle = tri.reshape(channels, 2 * half_t, t).transpose(1, 2, 0).astype(jnp.float32)
    tri_hat, tri_inv = normalize(triangle)
    onorm = (tri_hat * out_gain).astype(jnp.bfloat16)
    projected = jnp.einsum("ijc,cd->ijd", onorm, out_weight, preferred_element_type=jnp.float32)
    sig_gate = jax.nn.sigmoid(gate_out)
    cot_f = cotangent.astype(jnp.float32)
    dproj = (cot_f * sig_gate).astype(jnp.bfloat16)
    dgate = cot_f * projected * sig_gate * (1.0 - sig_gate)
    out_weight_local = jnp.einsum("ijc,ijd->cd", onorm, dproj, preferred_element_type=jnp.float32)
    donorm = jnp.einsum("ijd,cd->ijc", dproj, out_weight, preferred_element_type=jnp.float32)
    out_gain_local = jnp.sum(donorm * tri_hat, axis=(0, 1))
    dtri = layer_back(donorm * out_gain, tri_hat, tri_inv).astype(jnp.bfloat16)
    dtri_c = matrix(exchange(out_full(dtri)))
    dtri_rows = lax.dynamic_index_in_dim(
        dtri_c.reshape(rows, 2, half_t, cols * t), half, 1, keepdims=False
    ).reshape(rows * half_t, cols * t)
    dleft_c = jnp.einsum("kj,ij->ki", right_c, dtri_rows, preferred_element_type=jnp.float32)
    dright_c = jnp.einsum("ki,ij->kj", left_c, pick(dtri_c), preferred_element_type=jnp.float32)

    def back(x):
        x = x.astype(jnp.bfloat16).reshape(rows, t, cols, half_t)
        return x.transpose(0, 2, 1, 3).reshape(rows * cols, t * half_t)

    grads = exchange(jnp.concatenate([back(dleft_c), back(dright_c)], axis=1))

    def cells(x):
        x = x.reshape(channels, 2, t, half_t).transpose(2, 1, 3, 0)
        return x.reshape(t, t, channels).astype(jnp.float32)

    dleft = cells(grads[:, : t * half_t])
    dright = cells(grads[:, t * half_t :])
    dlin = jnp.concatenate(
        [
            dleft * mask_f * sig_left,
            dleft * mask_f * proj_left * sig_left * (1.0 - sig_left),
            dright * mask_f * sig_right,
            dright * mask_f * proj_right * sig_right * (1.0 - sig_right),
            dgate,
        ],
        axis=-1,
    ).astype(jnp.bfloat16)
    proj_local = jnp.einsum("ijc,ije->ce", zn, dlin, preferred_element_type=jnp.float32)
    dzn = jnp.einsum("ije,ce->ijc", dlin, proj_weight, preferred_element_type=jnp.float32)
    in_gain_local = jnp.sum(dzn * normed, axis=(0, 1))
    d_pair = layer_back(dzn * in_gain, normed, inverse)
    proj_sum, out_weight_sum, in_gain_sum, out_gain_sum = lax.psum(
        (proj_local, out_weight_local, in_gain_local, out_gain_local), ("row", "col")
    )
    return (
        d_pair,
        proj_sum / total,
        out_weight_sum / total,
        in_gain_sum / total,
        out_gain_sum / total,
    )


def solution(mesh):
    in_specs = (P("row", "col", None), P("row", "col"), P(), P(), P(), P(), P("row", "col", None))
    out_specs = (P("row", "col", None), P(), P(), P(), P())
    return jax.shard_map(body, mesh=mesh, in_specs=in_specs, out_specs=out_specs, check_vma=False)
```

profile of v0, /device:TPU:1, one launch (start us, length us, event | category | flops | bytes accessed | tf_op | source)
XLA Modules:
  0.0 653.1 jit_solution(1382171473351890345)
XLA Ops:
  28.2 17.0 %all-to-all-start = ((bf16[256,2,1024]{2,1,0:T(2,128)(2,1)}), bf16[256,2,1024]{2,1,0:T(2,128)(2,1)}, u32[]{:S(2)}, u32[]{:S(2)}) async-start(bf16[256,2,1024]{2,1,0:T(2,128)(2,1)} %reshape.165), calls=%async_computation | async-start | bytes 2097152 | tf_op jit(solution)/shard_map/all_to_all | solution.py:25
  45.2 31.4 %all-to-all-done = bf16[256,2,1024]{2,1,0:T(2,128)(2,1)} async-done(((bf16[256,2,1024]{2,1,0:T(2,128)(2,1)}), bf16[256,2,1024]{2,1,0:T(2,128)(2,1)}, u32[]{:S(2)}, u32[]{:S(2)}) %all-to-all-start) | async-done | bytes 1048608 | tf_op jit(solution)/shard_map/all_to_all | solution.py:25
  76.7 7.5 %reshape.166 = bf16[256,1,2048]{2,1,0:T(2,128)(2,1)} reshape(bf16[256,2,1024]{2,1,0:T(2,128)(2,1)} %all-to-all-done) | data formatting | bytes 2097152
  100.9 4.4 copy.69
  105.3 4.1 reshape_reshape.9
  123.0 20.4 %all_to_all.44 = bf16[256,2,256]{2,1,0:T(2,128)(2,1)S(1)} all-to-all(bf16[256,2,256]{2,1,0:T(2,128)(2,1)S(1)} %reshape.167), channel_id=1, replica_groups=mesh['row'=16,'col'=16] {'row','col'}, dimensions={0} | all-to-all | bytes 524288 | tf_op jit(solution)/shard_map/all_to_all | solution.py:25
  158.8 4.3 all_to_all.39
  163.2 5.6 reduce.5
  171.0 7.2 %all-to-all-start.2 = ((bf16[256,2,512]{2,1,0:T(2,128)(2,1)}), bf16[256,2,512]{2,1,0:T(2,128)(2,1)}, u32[]{:S(2)}, u32[]{:S(2)}) async-start(bf16[256,2,512]{2,1,0:T(2,128)(2,1)} %reshape.169), calls=%async_computation.2 | async-start | bytes 1048576 | tf_op jit(solution)/shard_map/all_to_all | solution.py:25
  182.0 4.1 reshape.149
  186.1 12.2 %all-to-all-done.2 = bf16[256,2,512]{2,1,0:T(2,128)(2,1)} async-done(((bf16[256,2,512]{2,1,0:T(2,128)(2,1)}), bf16[256,2,512]{2,1,0:T(2,128)(2,1)}, u32[]{:S(2)}, u32[]{:S(2)}) %all-to-all-start.2) | async-done | bytes 524320 | tf_op jit(solution)/shard_map/all_to_all | solution.py:25
  198.3 4.4 reshape.170
  202.7 4.9 reduce.1
  211.4 4.4 copy.80
  219.6 4.1 reshape_reshape.11
  245.6 5.1 reshape.152
  253.7 5.1 reshape.148
  265.6 6.8 %all-to-all-start.3 = ((bf16[256,2,512]{2,1,0:T(2,128)(2,1)}), bf16[256,2,512]{2,1,0:T(2,128)(2,1)}, u32[]{:S(2)}, u32[]{:S(2)}) async-start(bf16[256,2,512]{2,1,0:T(2,128)(2,1)} %reshape.171), calls=%async_computation.3 | async-start | bytes 1048576 | tf_op jit(solution)/shard_map/all_to_all | solution.py:25
  274.6 17.4 %all-to-all-done.3 = bf16[256,2,512]{2,1,0:T(2,128)(2,1)} async-done(((bf16[256,2,512]{2,1,0:T(2,128)(2,1)}), bf16[256,2,512]{2,1,0:T(2,128)(2,1)}, u32[]{:S(2)}, u32[]{:S(2)}) %all-to-all-start.3) | async-done | bytes 524320 | tf_op jit(solution)/shard_map/all_to_all | solution.py:25
  292.1 4.6 reshape.172
  302.9 4.5 copy.85
  311.1 4.5 copy.84
  323.3 72.4 %all-reduce = (f32[128]{0:T(128)S(1)}, f32[128]{0:T(128)S(1)}) all-reduce(f32[128]{0:T(128)S(1)} %get-tuple-element.7, f32[128]{0:T(128)S(1)} %get-tuple-element.5), channel_id=1, replica_groups=mesh['row'=16,'col'=16] {'row','col'}, use_global_device_ids=true, to_apply=%region_11.12 | all-reduce | flops 256 | bytes 2048 | tf_op jit(solution)/shard_map/psum | solution.py:112
  398.2 244.6 %all-reduce.4.cloned.1.call-done = (f32[128,640]{1,0:T(8,128)}, f32[128,128]{1,0:T(8,128)}) async-done(((f32[128,640]{1,0:T(8,128)}, f32[128,128]{1,0:T(8,128)}), (f32[128,640]{1,0:T(8,128)}, f32[128,128]{1,0:T(8,128)})) %all-reduce.4.cloned.1.call-update) | async-done | bytes 393232 | tf_op jit(solution)/shard_map/psum | solution.py:112
  (103 shorter events, 137.3 us)
Async XLA Ops:
  7.2 3.3 copy-start
  7.2 4.9 copy-start.5
  28.2 48.5 %all-to-all-start = ((bf16[256,2,1024]{2,1,0:T(2,128)(2,1)}), bf16[256,2,1024]{2,1,0:T(2,128)(2,1)}, u32[]{:S(2)}, u32[]{:S(2)}) async-start(bf16[256,2,1024]{2,1,0:T(2,128)(2,1)} %reshape.165), calls=%async_computation | async-start | bytes 2097152 | tf_op jit(solution)/shard_map/all_to_all | solution.py:25
  96.9 13.4 %copy-start.3 = (bf16[512,512]{1,0:T(8,128)(2,1)}, bf16[512,512]{1,0:T(8,128)(2,1)S(1)}, u32[]{:S(2)}) copy-start(bf16[512,512]{1,0:T(8,128)(2,1)S(1)} %reshape.141) | copy-start | bytes 1572868
  148.8 3.3 copy-start.7
  148.8 3.3 copy-start.9
  171.0 27.3 %all-to-all-start.2 = ((bf16[256,2,512]{2,1,0:T(2,128)(2,1)}), bf16[256,2,512]{2,1,0:T(2,128)(2,1)}, u32[]{:S(2)}, u32[]{:S(2)}) async-start(bf16[256,2,512]{2,1,0:T(2,128)(2,1)} %reshape.169), calls=%async_computation.2 | async-start | bytes 1048576 | tf_op jit(solution)/shard_map/all_to_all | solution.py:25
  265.6 26.4 %all-to-all-start.3 = ((bf16[256,2,512]{2,1,0:T(2,128)(2,1)}), bf16[256,2,512]{2,1,0:T(2,128)(2,1)}, u32[]{:S(2)}, u32[]{:S(2)}) async-start(bf16[256,2,512]{2,1,0:T(2,128)(2,1)} %reshape.171), calls=%async_computation.3 | async-start | bytes 1048576 | tf_op jit(solution)/shard_map/all_to_all | solution.py:25
  272.4 370.4 %all-reduce.4.cloned.1.call-start = ((), (), s32[]{:S(2)}) async-start(), calls=%async_computation.4 | async-start | bytes 786432 | tf_op jit(solution)/shard_map/psum | solution.py:112
  317.2 1.0 copy-start.6
  317.4 2.3 copy-start.1
  317.4 2.3 copy-start.8
  318.7 1.1 copy-start.4
  319.8 76.6 %copy-start.2 = (bf16[32,32,128]{2,1,0:T(8,128)(2,1)S(1)}, bf16[32,32,128]{2,1,0:T(8,128)(2,1)}, u32[]{:S(2)}) copy-start(bf16[32,32,128]{2,1,0:T(8,128)(2,1)} %param.7) | copy-start | bytes 786436
Sparse Core Ops, SparseCore 0:
  396.4 246.3 all-reduce.3
where the time goes:
time: 660 us; the launch traced here: 653 us
  waiting for transfers between devices  306 us (46%)
  local copies, waits for them, and re-layouts  153 us (23%)
  blocking collectives  92.9 us (14%)
  other arithmetic  40.9 us (6%)
  starting transfers between devices  31.1 us (5%)
  between operations  14.6 us (2%)
  matrix products  14.5 us (2%)
    psum x1, waiting for transfers between devices, body(): lax.psum((proj_local, out_weight_local, in_gain_local, out_gain_local), (...  245 us
    psum x1, blocking collectives, body(): lax.psum((proj_local, out_weight_local, in_gain_local, out_gain_local), (...  72.4 us
    all_to_all x3, waiting for transfers between devices, exchange(): return lax.all_to_all(x, AXES, split_axis=0, concat_axis=0, tiled=True)  61.1 us
    unnamed x34, local copies, waits for them, and re-layouts  31.1 us
    all_to_all x3, starting transfers between devices, exchange(): return lax.all_to_all(x, AXES, split_axis=0, concat_axis=0, tiled=True)  31 us
    all_to_all x7, other arithmetic, exchange(): return lax.all_to_all(x, AXES, split_axis=0, concat_axis=0, tiled=True)  23.7 us
    all_to_all x1, blocking collectives, exchange(): return lax.all_to_all(x, AXES, split_axis=0, concat_axis=0, tiled=True)  20.4 us
    transpose x5, local copies, waits for them, and re-layouts, matrix(): x.reshape(rows, cols, t, t).transpose(0, 2, 1, 3)  20.2 us
  transfers between devices with their start and end apart: 4, of which 4 were waited for; matrix products, arithmetic and copies ran while one was open for 2% of the time, Pallas kernels for 0%

commit v1 on v0

--- a/solution.py
+++ b/solution.py
@@ -109,8 +109,11 @@
     dzn = jnp.einsum("ije,ce->ijc", dlin, proj_weight, preferred_element_type=jnp.float32)
     in_gain_local = jnp.sum(dzn * normed, axis=(0, 1))
     d_pair = layer_back(dzn * in_gain, normed, inverse)
-    proj_sum, out_weight_sum, in_gain_sum, out_gain_sum = lax.psum(
-        (proj_local, out_weight_local, in_gain_local, out_gain_local), ("row", "col")
+    proj_sum, out_weight_sum, in_gain_sum, out_gain_sum = jax.lax.psum(
+        jax.lax.psum(
+            (proj_local, out_weight_local, in_gain_local, out_gain_local), axis_name="row"
+        ),
+        axis_name="col",
     )
     return (
         d_pair,

time: 660 us -> 683 us (1.035)
  waiting for transfers between devices: 306 us -> 337 us
  blocking collectives: 92.9 us -> 84.4 us
    psum x1 -> x2, waiting for transfers between devices: 245 us -> 275 us  [the longest x1 156 us: body(): jax.lax.psum(jax.lax.psum((proj_local, out_weight_local, in_gain_local, o...]
    psum x1 -> x2, blocking collectives: 72.4 us -> 64 us  [the longest x1 39.8 us: body(): jax.lax.psum(jax.lax.psum((proj_local, out_weight_local, in_gain_local, o...]
  transfers between devices with their start and end apart: 4 -> 5, of which waited for: 4 -> 5; matrix products, arithmetic and copies ran while one was open for 2% -> 2% of each run, Pallas kernels for 0% -> 0%
where the time goes in v1:
time: 683 us; the launch traced here: 676 us
  waiting for transfers between devices  337 us (49%)
  local copies, waits for them, and re-layouts  153 us (22%)
  blocking collectives  84.4 us (12%)
  other arithmetic  40.9 us (6%)
  starting transfers between devices  31.1 us (5%)
  matrix products  14.6 us (2%)
  between operations  14.6 us (2%)
    psum x1, waiting for transfers between devices, body(): jax.lax.psum(jax.lax.psum((proj_local, out_weight_local, in_gain_local, o...  156 us
    psum x1, waiting for transfers between devices, body(): jax.lax.psum((proj_local, out_weight_local, in_gain_local, out_gain_local...  119 us
    all_to_all x3, waiting for transfers between devices, exchange(): return lax.all_to_all(x, AXES, split_axis=0, concat_axis=0, tiled=True)  61.1 us
    psum x1, blocking collectives, body(): jax.lax.psum(jax.lax.psum((proj_local, out_weight_local, in_gain_local, o...  39.8 us
    unnamed x34, local copies, waits for them, and re-layouts  31.1 us
    all_to_all x3, starting transfers between devices, exchange(): return lax.all_to_all(x, AXES, split_axis=0, concat_axis=0, tiled=True)  31 us
    psum x1, blocking collectives, body(): jax.lax.psum((proj_local, out_weight_local, in_gain_local, out_gain_local...  24.2 us
    all_to_all x7, other arithmetic, exchange(): return lax.all_to_all(x, AXES, split_axis=0, concat_axis=0, tiled=True)  23.7 us
  transfers between devices with their start and end apart: 5, of which 5 were waited for; matrix products, arithmetic and copies ran while one was open for 2% of the time, Pallas kernels for 0%

profile of v1, /device:TPU:1, one launch (start us, length us, event | category | flops | bytes accessed | tf_op | source)
XLA Modules:
  0.0 675.6 jit_solution(1542144916520759817)
XLA Ops:
  28.2 17.0 %all-to-all-start = ((bf16[256,2,1024]{2,1,0:T(2,128)(2,1)}), bf16[256,2,1024]{2,1,0:T(2,128)(2,1)}, u32[]{:S(2)}, u32[]{:S(2)}) async-start(bf16[256,2,1024]{2,1,0:T(2,128)(2,1)} %reshape.165), calls=%async_computation | async-start | bytes 2097152 | tf_op jit(solution)/shard_map/all_to_all | solution.py:25
  45.2 31.4 %all-to-all-done = bf16[256,2,1024]{2,1,0:T(2,128)(2,1)} async-done(((bf16[256,2,1024]{2,1,0:T(2,128)(2,1)}), bf16[256,2,1024]{2,1,0:T(2,128)(2,1)}, u32[]{:S(2)}, u32[]{:S(2)}) %all-to-all-start) | async-done | bytes 1048608 | tf_op jit(solution)/shard_map/all_to_all | solution.py:25
  76.7 7.5 %reshape.166 = bf16[256,1,2048]{2,1,0:T(2,128)(2,1)} reshape(bf16[256,2,1024]{2,1,0:T(2,128)(2,1)} %all-to-all-done) | data formatting | bytes 2097152
  100.9 4.4 copy.69
  123.0 20.4 %all_to_all.44 = bf16[256,2,256]{2,1,0:T(2,128)(2,1)S(1)} all-to-all(bf16[256,2,256]{2,1,0:T(2,128)(2,1)S(1)} %reshape.167), channel_id=1, replica_groups=mesh['row'=16,'col'=16] {'row','col'}, dimensions={0} | all-to-all | bytes 524288 | tf_op jit(solution)/shard_map/all_to_all | solution.py:25
  158.8 4.3 all_to_all.39
  163.2 5.6 reduce.5
  171.0 7.2 %all-to-all-start.2 = ((bf16[256,2,512]{2,1,0:T(2,128)(2,1)}), bf16[256,2,512]{2,1,0:T(2,128)(2,1)}, u32[]{:S(2)}, u32[]{:S(2)}) async-start(bf16[256,2,512]{2,1,0:T(2,128)(2,1)} %reshape.169), calls=%async_computation.2 | async-start | bytes 1048576 | tf_op jit(solution)/shard_map/all_to_all | solution.py:25
  186.1 12.2 %all-to-all-done.2 = bf16[256,2,512]{2,1,0:T(2,128)(2,1)} async-done(((bf16[256,2,512]{2,1,0:T(2,128)(2,1)}), bf16[256,2,512]{2,1,0:T(2,128)(2,1)}, u32[]{:S(2)}, u32[]{:S(2)}) %all-to-all-start.2) | async-done | bytes 524320 | tf_op jit(solution)/shard_map/all_to_all | solution.py:25
  198.3 4.4 reshape.170
  202.7 4.9 reduce.1
  211.4 4.4 copy.80
  219.6 4.1 reshape_reshape.11
  245.6 5.1 reshape.152
  253.7 5.1 reshape.148
  265.6 6.8 %all-to-all-start.3 = ((bf16[256,2,512]{2,1,0:T(2,128)(2,1)}), bf16[256,2,512]{2,1,0:T(2,128)(2,1)}, u32[]{:S(2)}, u32[]{:S(2)}) async-start(bf16[256,2,512]{2,1,0:T(2,128)(2,1)} %reshape.171), calls=%async_computation.3 | async-start | bytes 1048576 | tf_op jit(solution)/shard_map/all_to_all | solution.py:25
  274.6 17.4 %all-to-all-done.3 = bf16[256,2,512]{2,1,0:T(2,128)(2,1)} async-done(((bf16[256,2,512]{2,1,0:T(2,128)(2,1)}), bf16[256,2,512]{2,1,0:T(2,128)(2,1)}, u32[]{:S(2)}, u32[]{:S(2)}) %all-to-all-start.3) | async-done | bytes 524320 | tf_op jit(solution)/shard_map/all_to_all | solution.py:25
  292.1 4.6 reshape.172
  302.9 4.5 copy.85
  311.1 4.5 copy.84
  323.4 24.2 %all-reduce.2 = (f32[128]{0:T(128)S(1)}, f32[128]{0:T(128)S(1)}) all-reduce(f32[128]{0:T(128)S(1)} %get-tuple-element.7, f32[128]{0:T(128)S(1)} %get-tuple-element.5), channel_id=1, replica_groups=mesh['row'=16,'col'=16] {'row'}, use_global_device_ids=true, to_apply=%region_13.14 | all-reduce | flops 256 | bytes 2048 | tf_op jit(solution)/shard_map/psum | solution.py:113
  347.5 39.8 %all-reduce = (f32[128]{0:T(128)S(1)}, f32[128]{0:T(128)S(1)}) all-reduce(f32[128]{0:T(128)S(1)} %get-tuple-element.15, f32[128]{0:T(128)S(1)} %get-tuple-element.16), channel_id=1, replica_groups=mesh['row'=16,'col'=16] {'col'}, use_global_device_ids=true, to_apply=%region_14.15 | all-reduce | flops 256 | bytes 2048 | tf_op jit(solution)/shard_map/psum | solution.py:112
  388.0 119.5 %all-reduce.9.cloned.1.call-done = (f32[128,640]{1,0:T(8,128)}, f32[128,128]{1,0:T(8,128)}) async-done(((f32[128,640]{1,0:T(8,128)}, f32[128,128]{1,0:T(8,128)}), (f32[128,640]{1,0:T(8,128)}, f32[128,128]{1,0:T(8,128)})) %all-reduce.9.cloned.1.call-update) | async-done | bytes 393232 | tf_op jit(solution)/shard_map/psum | solution.py:113
  509.4 155.9 %all-reduce.7.cloned.1.call-done = (f32[128,640]{1,0:T(8,128)}, f32[128,128]{1,0:T(8,128)}) async-done(((f32[128,640]{1,0:T(8,128)}, f32[128,128]{1,0:T(8,128)}), (f32[128,640]{1,0:T(8,128)}, f32[128,128]{1,0:T(8,128)})) %all-reduce.7.cloned.1.call-update) | async-done | bytes 393232 | tf_op jit(solution)/shard_map/psum | solution.py:112
  (107 shorter events, 145.6 us)
Async XLA Ops:
  7.2 3.3 copy-start
  7.2 4.9 copy-start.5
  28.2 48.5 %all-to-all-start = ((bf16[256,2,1024]{2,1,0:T(2,128)(2,1)}), bf16[256,2,1024]{2,1,0:T(2,128)(2,1)}, u32[]{:S(2)}, u32[]{:S(2)}) async-start(bf16[256,2,1024]{2,1,0:T(2,128)(2,1)} %reshape.165), calls=%async_computation | async-start | bytes 2097152 | tf_op jit(solution)/shard_map/all_to_all | solution.py:25
  96.9 13.4 %copy-start.3 = (bf16[512,512]{1,0:T(8,128)(2,1)}, bf16[512,512]{1,0:T(8,128)(2,1)S(1)}, u32[]{:S(2)}) copy-start(bf16[512,512]{1,0:T(8,128)(2,1)S(1)} %reshape.141) | copy-start | bytes 1572868
  148.8 3.3 copy-start.7
  148.8 3.3 copy-start.9
  171.0 27.3 %all-to-all-start.2 = ((bf16[256,2,512]{2,1,0:T(2,128)(2,1)}), bf16[256,2,512]{2,1,0:T(2,128)(2,1)}, u32[]{:S(2)}, u32[]{:S(2)}) async-start(bf16[256,2,512]{2,1,0:T(2,128)(2,1)} %reshape.169), calls=%async_computation.2 | async-start | bytes 1048576 | tf_op jit(solution)/shard_map/all_to_all | solution.py:25
  265.6 26.4 %all-to-all-start.3 = ((bf16[256,2,512]{2,1,0:T(2,128)(2,1)}), bf16[256,2,512]{2,1,0:T(2,128)(2,1)}, u32[]{:S(2)}, u32[]{:S(2)}) async-start(bf16[256,2,512]{2,1,0:T(2,128)(2,1)} %reshape.171), calls=%async_computation.3 | async-start | bytes 1048576 | tf_op jit(solution)/shard_map/all_to_all | solution.py:25
  272.4 235.0 %all-reduce.9.cloned.1.call-start = ((), (), s32[]{:S(2)}) async-start(), calls=%async_computation.5 | async-start | bytes 786432 | tf_op jit(solution)/shard_map/psum | solution.py:113
  317.2 1.0 copy-start.6
  317.4 2.3 copy-start.1
  317.4 2.3 copy-start.8
  318.7 1.1 copy-start.4
  321.2 186.8 %copy-start.2 = (bf16[32,32,128]{2,1,0:T(8,128)(2,1)S(1)}, bf16[32,32,128]{2,1,0:T(8,128)(2,1)}, u32[]{:S(2)}) copy-start(bf16[32,32,128]{2,1,0:T(8,128)(2,1)} %param.7) | copy-start | bytes 786436
  387.4 277.9 %all-reduce.7.cloned.1.call-start = ((), (), s32[]{:S(2)}) async-start(), calls=%async_computation.4 | async-start | bytes 786432 | tf_op jit(solution)/shard_map/psum | solution.py:112
Sparse Core Ops, SparseCore 0:
  387.5 119.8 all-reduce.8
  510.1 155.1 all-reduce.6
